TPU v7x, 256 devices: a whole 4x4x8 slice. The times are simulated.
256 devices in a mesh: branch: 64 (over x, z, core), sub: 4 (over y).
Axes of the slice: x: 4, y: 4, z: 8, core: 2. Of those that a mesh axis runs over, the one named last changes fastest.
Arguments:
- vectors: float32 [9216, 16, 128], P(('branch', 'sub')), may hold values from -6 to 6
- leaf_basis: float32 [9216, 64, 128], P(('branch', 'sub')), may hold values from -0.5 to 0.5
- near_index: int32 [9216, 3], P(('branch', 'sub')), may hold values from 0 to 9215, as said below
- near_blocks: float32 [9216, 3, 128, 128], P(('branch', 'sub')), may hold values from -0.3125 to 0.3125
- coupling_index: int32 [9216, 4], P(('branch', 'sub')), may hold values from 0 to 9215, as said below
- coupling_blocks: float32 [9216, 4, 64, 64], P(('branch', 'sub')), may hold values from -0.375 to 0.375
- leaf_transfer: float32 [9216, 64, 64], P(('branch', 'sub')), may hold values from -0.125 to 0.125
- cluster_transfer: float32 [256, 64, 64], P(('branch', 'sub')), may hold values from -0.375 to 0.375
- branch_index: int32 [64, 16], P('branch'), may hold values from 0 to 63, as said below
- branch_blocks: float32 [64, 16, 64, 64], P('branch'), may hold values from -0.1875 to 0.1875
Outputs:
- product: float32 [9216, 16, 128], P(('branch', 'sub'))
Inputs may be any that keep to these rules, and one draw needn't show every extreme that they name: `near_index`: entry 0 of row l is l itself; every entry of row l lies within 36 of l. `coupling_index`: every entry of row l lies within 36 of l. `branch_index`: the entries of a row are distinct and differ from the row's own branch cluster.
All inputs are finite; a program needn't handle non-finite values.
Results may differ from a plain program's by a relative error of at most 0.000067.
Values sent between devices are 32-bit elements; how exact they have to be, the bound alone decides.
A program may use at most 64 MiB of HBM per device.

v0:
```python
import jax
import jax.numpy as jnp
from jax import lax
from jax.sharding import PartitionSpec as P

highest = lax.Precision.HIGHEST


def with_halo(block, sides, width):
    for axis, dim in sides:
        count = lax.axis_size(axis)
        forward = [(i, i + 1) for i in range(count - 1)]
        backward = [(target, source) for source, target in forward]
        low = lax.ppermute(
            lax.slice_in_dim(block, block.shape[dim] - width, None, axis=dim), axis, forward
        )
        high = lax.ppermute(lax.slice_in_dim(block, 0, width, axis=dim), axis, backward)
        block = jnp.concatenate([low, block, high], axis=dim)
    return block


def per_device(
    vectors,
    leaf_basis,
    near_index,
    near_blocks,
    coupling_index,
    coupling_blocks,
    leaf_transfer,
    cluster_transfer,
    branch_index,
    branch_blocks,
):
    leaf_count = vectors.shape[0]
    coeffs = jnp.einsum("lrp,lvp->lvr", leaf_basis, vectors, precision=highest)
    wide_points = with_halo(vectors, ((("branch", "sub"), 0),), leaf_count)
    wide_coeffs = with_halo(coeffs, ((("branch", "sub"), 0),), leaf_count)
    anchor = lax.axis_index(("branch", "sub")) * leaf_count - leaf_count
    near_rows = jnp.take(wide_points, near_index - anchor, axis=0)
    near_part = jnp.einsum("lkpq,lkvq->lvp", near_blocks, near_rows, precision=highest)
    coupled_rows = jnp.take(wide_coeffs, coupling_index - anchor, axis=0)
    leaf_far = jnp.einsum("lkrs,lkvs->lvr", coupling_blocks, coupled_rows, precision=highest)
    cluster = jnp.einsum("crs,cvs->vr", leaf_transfer, coeffs, precision=highest)
    share = jnp.einsum("rt,vt->vr", cluster_transfer[0], cluster, precision=highest)
    branch_node = lax.psum(share, "sub")
    nodes = lax.all_gather(branch_node[None], "branch", axis=0, tiled=True)
    chosen = jnp.take(nodes, branch_index[0], axis=0)
    branch_far = jnp.einsum("krs,kvs->vr", branch_blocks[0], chosen, precision=highest)
    cluster_down = jnp.einsum("rt,vr->vt", cluster_transfer[0], branch_far, precision=highest)
    leaf_total = leaf_far + jnp.einsum(
        "crs,vr->cvs", leaf_transfer, cluster_down, precision=highest
    )
    return near_part + jnp.einsum("lrp,lvr->lvp", leaf_basis, leaf_total, precision=highest)


def solution(mesh):
    in_specs = (
        P(("branch", "sub"), None, None),
        P(("branch", "sub"), None, None),
        P(("branch", "sub"), None),
        P(("branch", "sub"), None, None, None),
        P(("branch", "sub"), None),
        P(("branch", "sub"), None, None, None),
        P(("branch", "sub"), None, None),
        P(("branch", "sub"), None, None),
        P("branch", None),
        P("branch", None, None, None),
    )
    out_specs = P(("branch", "sub"), None, None)
    return jax.shard_map(
        per_device, mesh=mesh, in_specs=in_specs, out_specs=out_specs, check_vma=False
    )
```

profile of v0, /device:TPU:1, one launch (start us, length us, event | category | flops | bytes accessed | tf_op | source)
XLA Modules:
  0.0 115.5 jit_solution(5684814676402167963)
XLA Ops:
  0.0 1.2 %copy-done = f32[36,64,128]{2,1,0:T(8,128)S(1)} copy-done((f32[36,64,128]{2,1,0:T(8,128)S(1)}, f32[36,64,128]{2,1,0:T(8,128)}, u32[]{:S(2)}) %copy-start) | copy-done | bytes 1179672
  1.3 2.9 %fusion.21 = f32[36,16,64]{2,1,0:T(8,128)S(1)} fusion(f32[36,16,128]{2,1,0:T(8,128)} %param.10, f32[36,64,128]{2,1,0:T(8,128)S(1)} %copy-done), kind=kOutput, calls=%fused_computation.41 | convolution fusion | flops 56623104 | bytes 1622016 | tf_op jit(solution)/shard_map/lrp,lvp->lvr/dot_general | solution.py:35
  4.2 6.2 %collective-permute-start.3 = (f32[36,16,64]{2,1,0:T(8,128)S(1)}, f32[36,16,64]{2,1,0:T(8,128)}, u32[]{:S(2)}, u32[]{:S(2)}) collective-permute-start(f32[36,16,64]{2,1,0:T(8,128)S(1)} %fusion.21), channel_id=1, source_target_pairs={{1,0},{2,1},{3,2},{4,3},{5,4},{6,5},{7,6},{8,7},{9,8},{10,9},{11,1... | collective-permute-start | bytes 442376 | tf_op jit(solution)/shard_map/ppermute | solution.py:17
  10.3 1.9 %collective-permute-start.2 = (f32[36,16,64]{2,1,0:T(8,128)S(1)}, f32[36,16,64]{2,1,0:T(8,128)}, u32[]{:S(2)}, u32[]{:S(2)}) collective-permute-start(f32[36,16,64]{2,1,0:T(8,128)S(1)} %fusion.21), channel_id=1, source_target_pairs={{0,1},{1,2},{2,3},{3,4},{4,5},{5,6},{6,7},{7,8},{8,9},{9,10},{10,1... | collective-permute-start | bytes 442376 | tf_op jit(solution)/shard_map/ppermute | solution.py:14
  12.3 4.9 %collective-permute-start.1 = (f32[36,16,128]{2,1,0:T(8,128)}, f32[36,16,128]{2,1,0:T(8,128)}, u32[]{:S(2)}, u32[]{:S(2)}) collective-permute-start(f32[36,16,128]{2,1,0:T(8,128)} %param.10), channel_id=1, source_target_pairs={{1,0},{2,1},{3,2},{4,3},{5,4},{6,5},{7,6},{8,7},{9,8},{10,9},{11,1... | collective-permute-start | bytes 884744 | tf_op jit(solution)/shard_map/ppermute | solution.py:17
  17.1 1.9 %collective-permute-start = (f32[36,16,128]{2,1,0:T(8,128)}, f32[36,16,128]{2,1,0:T(8,128)}, u32[]{:S(2)}, u32[]{:S(2)}) collective-permute-start(f32[36,16,128]{2,1,0:T(8,128)} %param.10), channel_id=1, source_target_pairs={{0,1},{1,2},{2,3},{3,4},{4,5},{5,6},{6,7},{7,8},{8,9},{9,10},{10,1... | collective-permute-start | bytes 884744 | tf_op jit(solution)/shard_map/ppermute | solution.py:14
  19.2 0.1 copy.21
  19.3 0.1 reshape.54
  19.4 0.1 copy.19
  19.5 0.1 reshape.46
  19.6 1.0 convolution_bitcast_fusion.2
  20.6 0.2 convolution_bitcast_fusion.5
  20.8 10.3 %psum.7 = f32[1,16,64]{2,1,0:T(8,128)S(1)} all-reduce(f32[1,16,64]{2,1,0:T(8,128)S(1)} %convolution_bitcast_fusion.5), channel_id=1, replica_groups=mesh['branch'=64,'sub'=4] {'sub'}, use_global_device_ids=true, to_apply=%region_0.1 | all-reduce | flops 1024 | bytes 8192 | tf_op jit(solution)/shard_map/psum | solution.py:45
  31.1 56.7 %all_gather.3 = f32[64,16,64]{2,1,0:T(8,128)S(1)} all-gather(f32[1,16,64]{2,1,0:T(8,128)S(1)} %psum.7), channel_id=1, replica_groups=mesh['branch'=64,'sub'=4] {'branch'}, dimensions={0}, use_global_device_ids=true | all-gather | bytes 266240 | tf_op jit(solution)/shard_map/all_gather | solution.py:46
  87.8 0.6 gather_fusion.2
  88.3 1.6 %convolution_bitcast_fusion.4 = f32[16,64]{1,0:T(8,128)S(1)} fusion(f32[1,16,64,64]{3,2,1,0:T(8,128)} %param.19, f32[16,16,64]{2,1,0:T(8,128)S(1)} %gather_fusion.2, pred[16]{0:T(512)(128)(4,1)S(1)} %compare_and_fusion), kind=kOutput, calls=%fused_computation.12 | convolution fusion | flops 12599296 | bytes 331792 | tf_op jit(solution)/shard_map/krs,kvs->vr/dot_general | solution.py:48
  90.0 0.7 copy.20
  90.7 0.7 copy.18
  91.4 0.1 convolution_bitcast_fusion.3
  91.5 0.0 collective-permute-done.3
  91.5 0.0 collective-permute-done.2
  91.5 1.1 pad_maximum_fusion.1
  92.7 1.8 %gather_fusion.1 = f32[144,16,64]{2,1,0:T(8,128)} fusion(f32[108,16,64]{2,1,0:T(8,128)S(1)} %pad_maximum_fusion.1, s32[1024]{0:T(1024)S(1)} %pad_clamp_fusion.1), kind=kCustom, calls=%fused_computation.1 | custom fusion | bytes 1180224 | tf_op jit(solution)/shard_map/jit(_take)/gather | solution.py:41
  94.5 6.7 %fusion.3 = f32[36,16,64]{2,1,0:T(8,128)S(1)} fusion(f32[36,4,64,64]{3,2,1,0:T(8,128)} %param.15, f32[36,4,16,64]{3,2,1,0:T(8,128)} %bitcast.46, pred[36,4]{1,0:T(8,128)(4,1)S(1)} %copy-done.4), kind=kOutput, calls=%fused_computation.8 | convolution fusion | flops 113393664 | bytes 3096720 | tf_op jit(solution)/shard_map/lkrs,lkvs->lvr/dot_general | solution.py:42
  101.2 0.7 fusion.2
  101.9 0.0 collective-permute-done.1
  101.9 0.0 collective-permute-done
  101.9 1.2 %pad_maximum_fusion = f32[108,16,128]{2,1,0:T(8,128)S(1)} fusion(f32[36,16,128]{2,1,0:T(8,128)} %collective-permute-done.1, f32[36,16,128]{2,1,0:T(8,128)} %param.10, f32[36,16,128]{2,1,0:T(8,128)} %collective-permute-done), kind=kLoop, calls=%fused_computation.14 | loop fusion | flops 442368 | bytes 1769472 | tf_op jit(solution)/shard_map/concatenate | solution.py:18
  103.1 0.0 copy-start.3
  103.1 0.7 gather_fusion
  103.8 9.8 %convolution_bitcast_fusion.1 = f32[36,16,128]{2,1,0:T(8,128)S(1)} fusion(f32[36,3,128,128]{3,2,1,0:T(8,128)} %param.13, f32[36,3,16,128]{3,2,1,0:T(8,128)S(1)} %bitcast.47, pred[36,3]{1,0:T(8,128)(4,1)S(1)} %copy-done.3), kind=kOutput, calls=%fused_computation.9 | convolution fusion | flops 339959808 | bytes 8257644 | tf_op jit(solution)/shard_map/lkpq,lkvq->lvp/dot_general | solution.py:40
  113.6 1.9 %convolution_add_fusion = f32[36,16,128]{2,1,0:T(8,128)} fusion(f32[36,16,128]{2,1,0:T(8,128)S(1)} %convolution_bitcast_fusion.1, f32[36,16,64]{2,1,0:T(8,128)S(1)} %fusion.2, f32[36,64,128]{2,1,0:T(8,128)S(1)} %copy-done), kind=kOutput, calls=%fused_computation.5 | convolution fusion | flops 56696832 | bytes 1916928 | tf_op jit(solution)/shard_map/lrp,lvr->lvp/dot_general | solution.py:53
  (21 shorter events, 0.1 us)
Async XLA Ops:
  0.0 1.3 %copy-start = (f32[36,64,128]{2,1,0:T(8,128)S(1)}, f32[36,64,128]{2,1,0:T(8,128)}, u32[]{:S(2)}) copy-start(f32[36,64,128]{2,1,0:T(8,128)} %param.11) | copy-start | bytes 3538948
  0.0 19.1 %copy-start.7 = (s32[1,16]{1,0:T(1,128)S(1)}, s32[1,16]{1,0:T(1,128)}, u32[]{:S(2)}) copy-start(s32[1,16]{1,0:T(1,128)} %param.18) | copy-start | bytes 196
  0.0 19.1 %copy-start.5 = (s32[36,3]{0,1:T(4,128)S(1)}, s32[36,3]{0,1:T(4,128)}, u32[]{:S(2)}) copy-start(s32[36,3]{0,1:T(4,128)} %param.12) | copy-start | bytes 1300
  0.0 19.1 %copy-start.6 = (s32[36,4]{0,1:T(4,128)S(1)}, s32[36,4]{0,1:T(4,128)}, u32[]{:S(2)}) copy-start(s32[36,4]{0,1:T(4,128)} %param.14) | copy-start | bytes 1732
  0.0 19.6 %copy-start.1 = (f32[36,64,64]{2,1,0:T(8,128)S(1)}, f32[36,64,64]{2,1,0:T(8,128)}, u32[]{:S(2)}) copy-start(f32[36,64,64]{2,1,0:T(8,128)} %param.16) | copy-start | bytes 1769476
  4.2 16.5 %copy-start.2 = (f32[1,64,64]{2,1,0:T(8,128)S(1)}, f32[1,64,64]{2,1,0:T(8,128)}, u32[]{:S(2)}) copy-start(f32[1,64,64]{2,1,0:T(8,128)} %param.17) | copy-start | bytes 49156
  4.2 87.3 %collective-permute-start.3 = (f32[36,16,64]{2,1,0:T(8,128)S(1)}, f32[36,16,64]{2,1,0:T(8,128)}, u32[]{:S(2)}, u32[]{:S(2)}) collective-permute-start(f32[36,16,64]{2,1,0:T(8,128)S(1)} %fusion.21), channel_id=1, source_target_pairs={{1,0},{2,1},{3,2},{4,3},{5,4},{6,5},{7,6},{8,7},{9,8},{10,9},{11,1... | collective-permute-start | bytes 442376 | tf_op jit(solution)/shard_map/ppermute | solution.py:17
  10.3 81.2 %collective-permute-start.2 = (f32[36,16,64]{2,1,0:T(8,128)S(1)}, f32[36,16,64]{2,1,0:T(8,128)}, u32[]{:S(2)}, u32[]{:S(2)}) collective-permute-start(f32[36,16,64]{2,1,0:T(8,128)S(1)} %fusion.21), channel_id=1, source_target_pairs={{0,1},{1,2},{2,3},{3,4},{4,5},{5,6},{6,7},{7,8},{8,9},{9,10},{10,1... | collective-permute-start | bytes 442376 | tf_op jit(solution)/shard_map/ppermute | solution.py:14
  12.3 89.6 %collective-permute-start.1 = (f32[36,16,128]{2,1,0:T(8,128)}, f32[36,16,128]{2,1,0:T(8,128)}, u32[]{:S(2)}, u32[]{:S(2)}) collective-permute-start(f32[36,16,128]{2,1,0:T(8,128)} %param.10), channel_id=1, source_target_pairs={{1,0},{2,1},{3,2},{4,3},{5,4},{6,5},{7,6},{8,7},{9,8},{10,9},{11,1... | collective-permute-start | bytes 884744 | tf_op jit(solution)/shard_map/ppermute | solution.py:17
  17.1 84.7 %collective-permute-start = (f32[36,16,128]{2,1,0:T(8,128)}, f32[36,16,128]{2,1,0:T(8,128)}, u32[]{:S(2)}, u32[]{:S(2)}) collective-permute-start(f32[36,16,128]{2,1,0:T(8,128)} %param.10), channel_id=1, source_target_pairs={{0,1},{1,2},{2,3},{3,4},{4,5},{5,6},{6,7},{7,8},{8,9},{9,10},{10,1... | collective-permute-start | bytes 884744 | tf_op jit(solution)/shard_map/ppermute | solution.py:14
  92.6 1.8 %copy-start.4 = (pred[36,4]{1,0:T(8,128)(4,1)S(1)}, pred[36,4]{1,0:T(8,128)(4,1)}, u32[]{:S(2)}) copy-start(pred[36,4]{1,0:T(8,128)(4,1)} %copy.20) | copy-start | bytes 436
  103.1 0.7 copy-start.3
where the time goes:
time: 116 us; the launch traced here: 115 us
  blocking collectives  67 us (58%)
  matrix products  24.9 us (21%)
  starting transfers between devices  14.9 us (13%)
  local copies, waits for them, and re-layouts  6.18 us (5%)
  other arithmetic  2.37 us (2%)
    all_gather x1, blocking collectives, per_device(): nodes = lax.all_gather(branch_node[None], 'branch', axis=0, tiled=True)  56.7 us
    ppermute x2, starting transfers between devices, with_halo(): lax.ppermute(lax.slice_in_dim(block, 0, width, axis=dim), axis, backward)  11 us
    psum x1, blocking collectives, per_device(): branch_node = lax.psum(share, 'sub')  10.3 us
    dot_general x1, matrix products, per_device(): jnp.einsum('lkpq,lkvq->lvp', near_blocks, near_rows, precision=highest)  9.8 us
    dot_general x1, matrix products, per_device(): jnp.einsum('lkrs,lkvs->lvr', coupling_blocks, coupled_rows, precision=hig...  6.69 us
    ppermute x2, starting transfers between devices, with_halo(): lax.ppermute(lax.slice_in_dim(block, block.shape[dim] - width, None, axis...  3.85 us
    dot_general x1, matrix products, per_device(): coeffs = jnp.einsum('lrp,lvp->lvr', leaf_basis, vectors, precision=highest)  2.89 us
  transfers between devices with their start and end apart: 4, of which 0 were waited for; matrix products, arithmetic and copies ran while one was open for 14% of the time, Pallas kernels for 0%

commit v1 on v0

--- a/solution.py
+++ b/solution.py
@@ -43,7 +43,11 @@
     cluster = jnp.einsum("crs,cvs->vr", leaf_transfer, coeffs, precision=highest)
     share = jnp.einsum("rt,vt->vr", cluster_transfer[0], cluster, precision=highest)
     branch_node = lax.psum(share, "sub")
-    nodes = lax.all_gather(branch_node[None], "branch", axis=0, tiled=True)
+    part = branch_node[None]
+    count_2 = lax.axis_size("branch")
+    shards = jnp.stack([part for _ in range(count_2)])
+    shards = lax.all_to_all(shards, "branch", split_axis=0, concat_axis=0)
+    nodes = jnp.concatenate(shards, axis=0)
     chosen = jnp.take(nodes, branch_index[0], axis=0)
     branch_far = jnp.einsum("krs,kvs->vr", branch_blocks[0], chosen, precision=highest)
     cluster_down = jnp.einsum("rt,vr->vt", cluster_transfer[0], branch_far, precision=highest)

time: 116 us -> 82.1 us (0.71)
  blocking collectives: 67 us -> 10.3 us
  starting transfers between devices: 14.9 us -> 29.5 us
  local copies, waits for them, and re-layouts: 6.18 us -> 10.9 us
  other arithmetic: 2.37 us -> 5.7 us
    all_gather x1 -> x0, blocking collectives: 56.7 us -> none  [per_device(): nodes = lax.all_gather(branch_node[None], 'branch', axis=0, tiled=True)]
    all_to_all x0 -> x1, starting transfers between devices: none -> 14.7 us  [per_device(): shards = lax.all_to_all(shards, 'branch', split_axis=0, concat_axis=0)]
    unnamed x16 -> x20, local copies, waits for them, and re-layouts: 1.27 us -> 3.98 us
    all_to_all x0 -> x1, other arithmetic: none -> 2.22 us  [per_device(): shards = lax.all_to_all(shards, 'branch', split_axis=0, concat_axis=0)]
  transfers between devices with their start and end apart: 4 -> 5, of which waited for: 0 -> 0; matrix products, arithmetic and copies ran while one was open for 14% -> 33% of each run, Pallas kernels for 0% -> 0%
where the time goes in v1:
time: 82.1 us; the launch traced here: 81.6 us
  starting transfers between devices  29.5 us (36%)
  matrix products  24.8 us (30%)
  local copies, waits for them, and re-layouts  10.9 us (13%)
  blocking collectives  10.3 us (13%)
  other arithmetic  5.7 us (7%)
    all_to_all x1, starting transfers between devices, per_device(): shards = lax.all_to_all(shards, 'branch', split_axis=0, concat_axis=0)  14.7 us
    ppermute x2, starting transfers between devices, with_halo(): lax.ppermute(lax.slice_in_dim(block, 0, width, axis=dim), axis, backward)  11 us
    psum x1, blocking collectives, per_device(): branch_node = lax.psum(share, 'sub')  10.3 us
    dot_general x1, matrix products, per_device(): jnp.einsum('lkpq,lkvq->lvp', near_blocks, near_rows, precision=highest)  9.77 us
    dot_general x1, matrix products, per_device(): jnp.einsum('lkrs,lkvs->lvr', coupling_blocks, coupled_rows, precision=hig...  6.7 us
    unnamed x20, local copies, waits for them, and re-layouts  3.98 us
    ppermute x2, starting transfers between devices, with_halo(): lax.ppermute(lax.slice_in_dim(block, block.shape[dim] - width, None, axis...  3.85 us
    dot_general x1, matrix products, per_device(): coeffs = jnp.einsum('lrp,lvp->lvr', leaf_basis, vectors, precision=highest)  2.89 us
  transfers between devices with their start and end apart: 5, of which 0 were waited for; matrix products, arithmetic and copies ran while one was open for 33% of the time, Pallas kernels for 0%

profile of v1, /device:TPU:1, one launch (start us, length us, event | category | flops | bytes accessed | tf_op | source)
XLA Modules:
  0.0 81.6 jit_solution(13903362835455736145)
XLA Ops:
  0.0 1.3 %copy-done = f32[36,64,128]{2,1,0:T(8,128)S(1)} copy-done((f32[36,64,128]{2,1,0:T(8,128)S(1)}, f32[36,64,128]{2,1,0:T(8,128)}, u32[]{:S(2)}) %copy-start) | copy-done | bytes 1179672
  1.3 2.9 %fusion.22 = f32[36,16,64]{2,1,0:T(8,128)S(1)} fusion(f32[36,16,128]{2,1,0:T(8,128)} %param.10, f32[36,64,128]{2,1,0:T(8,128)S(1)} %copy-done), kind=kOutput, calls=%fused_computation.41 | convolution fusion | flops 56623104 | bytes 1622016 | tf_op jit(solution)/shard_map/lrp,lvp->lvr/dot_general | solution.py:35
  4.2 6.2 %collective-permute-start.3 = (f32[36,16,64]{2,1,0:T(8,128)S(1)}, f32[36,16,64]{2,1,0:T(8,128)S(1)}, u32[]{:S(2)}, u32[]{:S(2)}) collective-permute-start(f32[36,16,64]{2,1,0:T(8,128)S(1)} %fusion.22), channel_id=1, source_target_pairs={{1,0},{2,1},{3,2},{4,3},{5,4},{6,5},{7,6},{8,7},{9,8},{10,9},{11,1... | collective-permute-start | bytes 442376 | tf_op jit(solution)/shard_map/ppermute | solution.py:17
  10.3 1.9 %collective-permute-start.2 = (f32[36,16,64]{2,1,0:T(8,128)S(1)}, f32[36,16,64]{2,1,0:T(8,128)}, u32[]{:S(2)}, u32[]{:S(2)}) collective-permute-start(f32[36,16,64]{2,1,0:T(8,128)S(1)} %fusion.22), channel_id=1, source_target_pairs={{0,1},{1,2},{2,3},{3,4},{4,5},{5,6},{6,7},{7,8},{8,9},{9,10},{10,1... | collective-permute-start | bytes 442376 | tf_op jit(solution)/shard_map/ppermute | solution.py:14
  12.3 4.9 %collective-permute-start.1 = (f32[36,16,128]{2,1,0:T(8,128)}, f32[36,16,128]{2,1,0:T(8,128)}, u32[]{:S(2)}, u32[]{:S(2)}) collective-permute-start(f32[36,16,128]{2,1,0:T(8,128)} %param.10), channel_id=1, source_target_pairs={{1,0},{2,1},{3,2},{4,3},{5,4},{6,5},{7,6},{8,7},{9,8},{10,9},{11,1... | collective-permute-start | bytes 884744 | tf_op jit(solution)/shard_map/ppermute | solution.py:17
  17.1 1.9 %collective-permute-start = (f32[36,16,128]{2,1,0:T(8,128)}, f32[36,16,128]{2,1,0:T(8,128)}, u32[]{:S(2)}, u32[]{:S(2)}) collective-permute-start(f32[36,16,128]{2,1,0:T(8,128)} %param.10), channel_id=1, source_target_pairs={{0,1},{1,2},{2,3},{3,4},{4,5},{5,6},{6,7},{7,8},{8,9},{9,10},{10,1... | collective-permute-start | bytes 884744 | tf_op jit(solution)/shard_map/ppermute | solution.py:14
  19.1 1.0 %convolution_bitcast_fusion.2 = f32[16,64]{1,0:T(8,128)S(1)} fusion(f32[36,16,64]{2,1,0:T(8,128)S(1)} %fusion.22, f32[36,64,64]{2,1,0:T(8,128)S(1)} %copy-done.1), kind=kOutput, calls=%fused_computation.10 | convolution fusion | flops 28311552 | bytes 741376 | tf_op jit(solution)/shard_map/crs,cvs->vr/dot_general | solution.py:43
  20.1 0.1 fusion.16
  20.3 10.3 %psum.7 = f32[16,64]{1,0:T(8,128)S(1)} all-reduce(f32[16,64]{1,0:T(8,128)S(1)} %fusion.16), channel_id=1, replica_groups=mesh['branch'=64,'sub'=4] {'sub'}, use_global_device_ids=true, to_apply=%region_0.1 | all-reduce | flops 1024 | bytes 8192 | tf_op jit(solution)/shard_map/psum | solution.py:45
  30.6 1.0 %reshape.83 = f32[64,1,1024]{2,1,0:T(1,128)} reshape(f32[64,1,16,64]{3,2,1,0:T(8,128)S(1)} %stack.3) | data formatting | bytes 524288
  31.6 14.7 %all-to-all-start = ((f32[64,1,1024]{2,1,0:T(1,128)}), f32[64,1,1024]{2,1,0:T(1,128)}, u32[]{:S(2)}, u32[]{:S(2)}) async-start(f32[64,1,1024]{2,1,0:T(1,128)} %reshape.83), calls=%async_computation | async-start | bytes 524288 | tf_op jit(solution)/shard_map/all_to_all | solution.py:49
  46.4 0.5 compare_and_fusion
  46.9 0.6 pad_clamp_fusion
  47.5 0.1 copy.17
  47.8 0.7 copy.16
  48.5 0.1 copy.14
  48.7 0.1 reshape.52
  48.8 0.7 copy-done.2
  49.5 1.1 %pad_maximum_fusion.1 = f32[108,16,64]{2,1,0:T(8,128)S(1)} fusion(f32[36,16,64]{2,1,0:T(8,128)} %copy-done.2, f32[36,16,64]{2,1,0:T(8,128)S(1)} %fusion.22, f32[36,16,64]{2,1,0:T(8,128)} %collective-permute-done.2), kind=kLoop, calls=%fused_computation.14 | loop fusion | flops 221184 | bytes 884736 | tf_op jit(solution)/shard_map/concatenate | solution.py:18
  50.7 1.8 %gather_fusion.1 = f32[144,16,64]{2,1,0:T(8,128)} fusion(f32[108,16,64]{2,1,0:T(8,128)S(1)} %pad_maximum_fusion.1, s32[1024]{0:T(1024)S(1)} %pad_clamp_fusion.1), kind=kCustom, calls=%fused_computation.1 | custom fusion | bytes 1180224 | tf_op jit(solution)/shard_map/jit(_take)/gather | solution.py:41
  52.5 6.7 %fusion.3 = f32[36,16,64]{2,1,0:T(8,128)S(1)} fusion(f32[36,4,64,64]{3,2,1,0:T(8,128)} %param.15, f32[36,4,16,64]{3,2,1,0:T(8,128)} %bitcast.45, pred[36,4]{1,0:T(8,128)(4,1)} %copy.16), kind=kOutput, calls=%fused_computation.8 | convolution fusion | flops 113393664 | bytes 3096720 | tf_op jit(solution)/shard_map/lkrs,lkvs->lvr/dot_general | solution.py:42
  59.2 1.2 %pad_maximum_fusion = f32[108,16,128]{2,1,0:T(8,128)S(1)} fusion(f32[36,16,128]{2,1,0:T(8,128)} %collective-permute-done.1, f32[36,16,128]{2,1,0:T(8,128)} %param.10, f32[36,16,128]{2,1,0:T(8,128)} %collective-permute-done), kind=kLoop, calls=%fused_computation.13 | loop fusion | flops 442368 | bytes 1769472 | tf_op jit(solution)/shard_map/concatenate | solution.py:18
  60.4 1.6 %gather_fusion = f32[108,16,128]{2,1,0:T(8,128)} fusion(f32[108,16,128]{2,1,0:T(8,128)S(1)} %pad_maximum_fusion, s32[1024]{0:T(1024)S(1)} %pad_clamp_fusion.2), kind=kCustom, calls=%fused_computation | custom fusion | bytes 1769904 | tf_op jit(solution)/shard_map/jit(_take)/gather | solution.py:39
  62.0 9.8 %convolution_bitcast_fusion.1 = f32[36,16,128]{2,1,0:T(8,128)S(1)} fusion(f32[36,3,128,128]{3,2,1,0:T(8,128)} %param.13, f32[36,3,16,128]{3,2,1,0:T(8,128)} %bitcast.46, pred[36,3]{1,0:T(8,128)(4,1)S(1)} %copy.14), kind=kOutput, calls=%fused_computation.9 | convolution fusion | flops 339959808 | bytes 8257644 | tf_op jit(solution)/shard_map/lkpq,lkvq->lvp/dot_general | solution.py:40
  71.9 0.5 broadcast.52
  72.4 2.2 %reduce = f32[64,1024]{1,0:T(8,128)S(1)} reduce(f32[64,1,1024]{2,1,0:T(1,128)} %all-to-all-done, f32[]{:T(128)} %broadcast.52), dimensions={1}, to_apply=%all_to_all.3.reduce_sub_computation | reduce | bytes 524292 | tf_op jit(solution)/shard_map/all_to_all | solution.py:49
  74.6 0.9 %reshape.84 = f32[64,1,16,64]{3,2,1,0:T(8,128)} reshape(f32[64,1024]{1,0:T(8,128)S(1)} %reduce) | data formatting | bytes 524288
  75.5 1.7 %gather_fusion.2 = f32[16,16,64]{2,1,0:T(8,128)S(1)} fusion(f32[64,16,64]{2,1,0:T(8,128)} %bitcast.47, s32[1024]{0:T(1024)} %pad_clamp_fusion), kind=kCustom, calls=%fused_computation.2 | custom fusion | bytes 131136 | tf_op jit(solution)/shard_map/jit(_take)/gather | solution.py:51
  77.3 1.6 %convolution_bitcast_fusion.4 = f32[16,64]{1,0:T(8,128)S(1)} fusion(f32[1,16,64,64]{3,2,1,0:T(8,128)} %param.19, f32[16,16,64]{2,1,0:T(8,128)S(1)} %gather_fusion.2, pred[16]{0:T(512)(128)(4,1)S(1)} %copy-done.7), kind=kOutput, calls=%fused_computation.12 | convolution fusion | flops 12599296 | bytes 331792 | tf_op jit(solution)/shard_map/krs,kvs->vr/dot_general | solution.py:52
  78.9 0.1 convolution_bitcast_fusion.3
  79.0 0.7 fusion.2
  79.7 1.8 %convolution_add_fusion = f32[36,16,128]{2,1,0:T(8,128)} fusion(f32[36,16,128]{2,1,0:T(8,128)S(1)} %convolution_bitcast_fusion.1, f32[36,16,64]{2,1,0:T(8,128)S(1)} %fusion.2, f32[36,64,128]{2,1,0:T(8,128)S(1)} %copy-done), kind=kOutput, calls=%fused_computation.5 | convolution fusion | flops 56696832 | bytes 1916928 | tf_op jit(solution)/shard_map/lrp,lvr->lvp/dot_general | solution.py:57
  (29 shorter events, 0.3 us)
Async XLA Ops:
  0.0 1.3 %copy-start = (f32[36,64,128]{2,1,0:T(8,128)S(1)}, f32[36,64,128]{2,1,0:T(8,128)}, u32[]{:S(2)}) copy-start(f32[36,64,128]{2,1,0:T(8,128)} %param.11) | copy-start | bytes 3538948
  0.0 19.1 %copy-start.1 = (f32[36,64,64]{2,1,0:T(8,128)S(1)}, f32[36,64,64]{2,1,0:T(8,128)}, u32[]{:S(2)}) copy-start(f32[36,64,64]{2,1,0:T(8,128)} %param.16) | copy-start | bytes 1769476
  4.2 15.9 %copy-start.3 = (f32[1,64,64]{2,1,0:T(8,128)S(1)}, f32[1,64,64]{2,1,0:T(8,128)}, u32[]{:S(2)}) copy-start(f32[1,64,64]{2,1,0:T(8,128)} %param.17) | copy-start | bytes 49156
  4.2 44.6 %collective-permute-start.3 = (f32[36,16,64]{2,1,0:T(8,128)S(1)}, f32[36,16,64]{2,1,0:T(8,128)S(1)}, u32[]{:S(2)}, u32[]{:S(2)}) collective-permute-start(f32[36,16,64]{2,1,0:T(8,128)S(1)} %fusion.22), channel_id=1, source_target_pairs={{1,0},{2,1},{3,2},{4,3},{5,4},{6,5},{7,6},{8,7},{9,8},{10,9},{11,1... | collective-permute-start | bytes 442376 | tf_op jit(solution)/shard_map/ppermute | solution.py:17
  10.3 39.2 %collective-permute-start.2 = (f32[36,16,64]{2,1,0:T(8,128)S(1)}, f32[36,16,64]{2,1,0:T(8,128)}, u32[]{:S(2)}, u32[]{:S(2)}) collective-permute-start(f32[36,16,64]{2,1,0:T(8,128)S(1)} %fusion.22), channel_id=1, source_target_pairs={{0,1},{1,2},{2,3},{3,4},{4,5},{5,6},{6,7},{7,8},{8,9},{9,10},{10,1... | collective-permute-start | bytes 442376 | tf_op jit(solution)/shard_map/ppermute | solution.py:14
  12.3 46.9 %collective-permute-start.1 = (f32[36,16,128]{2,1,0:T(8,128)}, f32[36,16,128]{2,1,0:T(8,128)}, u32[]{:S(2)}, u32[]{:S(2)}) collective-permute-start(f32[36,16,128]{2,1,0:T(8,128)} %param.10), channel_id=1, source_target_pairs={{1,0},{2,1},{3,2},{4,3},{5,4},{6,5},{7,6},{8,7},{9,8},{10,9},{11,1... | collective-permute-start | bytes 884744 | tf_op jit(solution)/shard_map/ppermute | solution.py:17
  17.1 42.1 %collective-permute-start = (f32[36,16,128]{2,1,0:T(8,128)}, f32[36,16,128]{2,1,0:T(8,128)}, u32[]{:S(2)}, u32[]{:S(2)}) collective-permute-start(f32[36,16,128]{2,1,0:T(8,128)} %param.10), channel_id=1, source_target_pairs={{0,1},{1,2},{2,3},{3,4},{4,5},{5,6},{6,7},{7,8},{8,9},{9,10},{10,1... | collective-permute-start | bytes 884744 | tf_op jit(solution)/shard_map/ppermute | solution.py:14
  20.1 26.3 %copy-start.8 = (s32[1,16]{1,0:T(1,128)S(1)}, s32[1,16]{1,0:T(1,128)}, u32[]{:S(2)}) copy-start(s32[1,16]{1,0:T(1,128)} %param.18) | copy-start | bytes 196
  20.1 26.8 %copy-start.5 = (s32[36,3]{0,1:T(4,128)S(1)}, s32[36,3]{0,1:T(4,128)}, u32[]{:S(2)}) copy-start(s32[36,3]{0,1:T(4,128)} %param.12) | copy-start | bytes 1300
  20.1 26.8 %copy-start.6 = (s32[36,4]{0,1:T(4,128)S(1)}, s32[36,4]{0,1:T(4,128)}, u32[]{:S(2)}) copy-start(s32[36,4]{0,1:T(4,128)} %param.14) | copy-start | bytes 1732
  31.6 40.2 %all-to-all-start = ((f32[64,1,1024]{2,1,0:T(1,128)}), f32[64,1,1024]{2,1,0:T(1,128)}, u32[]{:S(2)}, u32[]{:S(2)}) async-start(f32[64,1,1024]{2,1,0:T(1,128)} %reshape.83), calls=%async_computation | async-start | bytes 524288 | tf_op jit(solution)/shard_map/all_to_all | solution.py:49
  48.8 0.7 copy-start.2
  71.8 5.4 %copy-start.7 = (pred[16]{0:T(512)(128)(4,1)S(1)}, pred[16]{0:T(512)(128)(4,1)}, u32[]{:S(2)}) copy-start(pred[16]{0:T(512)(128)(4,1)} %compare_and_fusion) | copy-start | bytes 52
  71.8 7.0 %copy-start.4 = (f32[1,64,64]{2,1,0:T(8,128)S(1)}, f32[1,64,64]{2,1,0:T(8,128)}, u32[]{:S(2)}) copy-start(f32[1,64,64]{2,1,0:T(8,128)} %param.17) | copy-start | bytes 49156
